TPU v7x, 128 devices: a whole 4x4x4 slice. The times are simulated.
128 devices in a mesh: fsdp: 16 (over y, x), sp: 8 (over z, core).
Axes of the slice: x: 4, y: 4, z: 4, core: 2. Of those that a mesh axis runs over, the one named last changes fastest.
Arguments:
- tokens: bfloat16 [16384, 1024], P(('fsdp', 'sp')), may hold values from -6 to 6
- segments: int32 [16, 1024], P('fsdp'), may hold values from 0 to 3, never falling along the last dimension, each value on 1 to 512 neighbouring positions
- top_idx: int32 [16384, 8], P(('fsdp', 'sp')), may hold values from 0 to 15, all different within a row; in each aligned block of 128 rows (0 to 127, 128 to 255, ...) at most 128 rows name the same one
- cotangent: bfloat16 [16384, 1024], P(('fsdp', 'sp')), may hold values from -6 to 6
- norm1_gain: bfloat16 [1024], P(('fsdp', 'sp')), may hold values from 0.099609375 to 1.8984375
- qkv_weight: bfloat16 [1024, 2048], P(('fsdp', 'sp')), may hold values from -0.1875 to 0.1875
- out_weight: bfloat16 [1024, 1024], P(('fsdp', 'sp')), may hold values from -4 to 4
- norm2_gain: bfloat16 [1024], P(('fsdp', 'sp')), may hold values from 0.099609375 to 1.8984375
- router_weight: bfloat16 [1024, 16], P(('fsdp', 'sp')), may hold values from -0.375 to 0.375
- expert_in: bfloat16 [16, 1024, 1024], P('sp', 'fsdp'), may hold values from -0.1875 to 0.1875
- expert_out: bfloat16 [16, 1024, 512], P('sp', 'fsdp'), may hold values from -2 to 2
Outputs:
- block_out: float32 [16384, 1024], P(('fsdp', 'sp'))
- input_grad: float32 [16384, 1024], P(('fsdp', 'sp'))
- norm1_gain_grad: float32 [1024], P(('fsdp', 'sp'))
- qkv_weight_grad: float32 [1024, 2048], P(('fsdp', 'sp'))
- out_weight_grad: float32 [1024, 1024], P(('fsdp', 'sp'))
- norm2_gain_grad: float32 [1024], P(('fsdp', 'sp'))
- router_weight_grad: float32 [1024, 16], P(('fsdp', 'sp'))
- expert_in_grad: float32 [16, 1024, 1024], P('sp', 'fsdp')
- expert_out_grad: float32 [16, 1024, 512], P('sp', 'fsdp')
Inputs may be any that keep to these rules, and one draw needn't show every extreme that they name: `top_idx`: the rows of one device name each expert at most 128 times; the 8 numbers of a row differ. `segments`: each sequence is cut into 4 documents of consecutive positions numbered upward from 0; the longest has 512 positions.
All inputs are finite; a program needn't handle non-finite values.
Results may differ from a plain program's by a relative error of at most 0.02.
Values may be sent and summed in bfloat16 or wider, within the bound.
A program may use at most 128 MiB of HBM per device.

v0:
```python
import jax
import jax.numpy as jnp
from jax import lax
from jax.sharding import PartitionSpec as P

HQ = 16
KEY_VALUE_HEADS = 8
HEAD_SIZE = 64
E = 16


EPSILON = 1e-06
RESIDUAL = 0.22


def rope_tables(positions):
    frequency = 10000.0 ** (-2.0 * jnp.arange(HEAD_SIZE // 2, dtype=jnp.float32) / HEAD_SIZE)
    angles = positions[:, None] * frequency[None, :]
    return (jnp.cos(angles), jnp.sin(angles))


def rotary_apply(value_rows, cosine_table, sine_table):
    half_width = value_rows.shape[-1] // 2
    first_half = value_rows[..., :half_width]
    second_half = value_rows[..., half_width:]
    cos_rows = cosine_table[:, None, :]
    sin_rows = sine_table[:, None, :]
    return jnp.concatenate(
        [
            first_half * cos_rows - second_half * sin_rows,
            second_half * cos_rows + first_half * sin_rows,
        ],
        -1,
    )


def rms_norm(value_rows, gain):
    return (
        value_rows
        * lax.rsqrt(jnp.mean(value_rows * value_rows, -1, keepdims=True) + EPSILON)
        * gain
    )


def slot_table(chosen_experts):
    expert_of = chosen_experts.reshape(-1)
    one_hot = (expert_of[:, None] == jnp.arange(E, dtype=jnp.int32)[None, :]).astype(jnp.int32)
    earlier = jnp.cumsum(one_hot, 0) - one_hot
    slot_rank = jnp.sum(earlier * one_hot, 1)
    return (expert_of, slot_rank)


def expert_forward(routed, weights_in, weights_out):
    hidden_units = weights_out.shape[2]
    pre_act = jnp.einsum("grd,gdf->grf", routed, weights_in, preferred_element_type=jnp.float32)
    activated = (jax.nn.silu(pre_act[..., :hidden_units]) * pre_act[..., hidden_units:]).astype(
        jnp.bfloat16
    )
    produced = jnp.einsum(
        "grf,gdf->grd", activated, weights_out, preferred_element_type=jnp.float32
    ).astype(jnp.bfloat16)
    return (pre_act, activated, produced)


def down_backward(grad_result, weights_out):
    return jnp.einsum("grd,gdf->grf", grad_result, weights_out, preferred_element_type=jnp.float32)


def expert_backward(pre_act, weights_in, grad_act):
    hidden_units = grad_act.shape[2]
    gate_part = pre_act[..., :hidden_units]
    up_part = pre_act[..., hidden_units:]
    sigmoid = jax.nn.sigmoid(gate_part)
    grad_gate = grad_act * up_part * sigmoid * (1.0 + gate_part * (1.0 - sigmoid))
    grad_up = grad_act * gate_part * sigmoid
    grad_pre = jnp.concatenate([grad_gate, grad_up], -1).astype(jnp.bfloat16)
    grad_rows = jnp.einsum(
        "grf,gdf->grd", grad_pre, weights_in, preferred_element_type=jnp.float32
    ).astype(jnp.bfloat16)
    return (grad_rows, grad_pre)


def weight_grads(routed, activated, grad_pre, grad_result):
    grad_inner = jnp.einsum("grd,grf->gdf", routed, grad_pre, preferred_element_type=jnp.float32)
    grad_outer = jnp.einsum(
        "grd,grf->gdf", grad_result, activated, preferred_element_type=jnp.float32
    )
    return (grad_inner, grad_outer)


def shards(
    tokens,
    segments,
    top_idx,
    cotangent,
    norm1_gain,
    qkv_weight,
    out_weight,
    norm2_gain,
    router_weight,
    expert_in,
    expert_out,
):
    sequence_parallel_count = lax.axis_size("sp")
    sp_index = lax.axis_index("sp")
    count_of_rows = tokens.shape[0]
    seq_len = count_of_rows * sequence_parallel_count
    width = tokens.shape[1]
    top_count = top_idx.shape[1]
    capacity = 2 * count_of_rows * top_count // E
    query_span_width = HQ * HEAD_SIZE
    key_span_width = KEY_VALUE_HEADS * HEAD_SIZE
    local_width = query_span_width // sequence_parallel_count
    local_key_value = KEY_VALUE_HEADS // sequence_parallel_count
    score_scale = HEAD_SIZE ** (-0.5)
    span = min(512, seq_len)
    block_count = seq_len // span
    gain_one, gain_two, qkv_full, out_full, router_full = (
        lax.all_gather(norm1_gain, ("fsdp", "sp"), axis=0, tiled=True),
        lax.all_gather(norm2_gain, ("fsdp", "sp"), axis=0, tiled=True),
        lax.all_gather(qkv_weight, ("fsdp", "sp"), axis=0, tiled=True),
        lax.all_gather(out_weight, ("fsdp", "sp"), axis=0, tiled=True),
        lax.all_gather(router_weight, ("fsdp", "sp"), axis=0, tiled=True),
    )
    experts_in, experts_out = (
        lax.all_gather(expert_in, "fsdp", axis=1, tiled=True),
        lax.all_gather(expert_out, "fsdp", axis=1, tiled=True),
    )
    hidden_in = tokens.astype(jnp.float32)
    normed_one, norm_one_pull = jax.vjp(rms_norm, hidden_in, gain_one.astype(jnp.float32))
    normed_one = normed_one.astype(jnp.bfloat16)
    projected_rows = jnp.dot(normed_one, qkv_full, preferred_element_type=jnp.float32)
    positions = (sp_index * count_of_rows + jnp.arange(count_of_rows, dtype=jnp.int32)).astype(
        jnp.float32
    )
    cosine_table, sine_table = rope_tables(positions)

    def rope_pair(query_part, key_part):
        return (
            rotary_apply(query_part, cosine_table, sine_table),
            rotary_apply(key_part, cosine_table, sine_table),
        )

    (rot_query, rot_key), rope_pull = jax.vjp(
        rope_pair,
        projected_rows[:, :query_span_width].reshape(count_of_rows, HQ, HEAD_SIZE),
        projected_rows[:, query_span_width : query_span_width + key_span_width].reshape(
            count_of_rows, KEY_VALUE_HEADS, HEAD_SIZE
        ),
    )
    value_portion = projected_rows[:, query_span_width + key_span_width :].reshape(
        count_of_rows, KEY_VALUE_HEADS, 1, HEAD_SIZE
    )
    packed_kv = (
        jnp.concatenate([rot_key[:, :, None, :], value_portion], 2)
        .astype(jnp.bfloat16)
        .reshape(count_of_rows, query_span_width)
    )
    outgoing = jnp.stack(
        [rot_query.astype(jnp.bfloat16).reshape(count_of_rows, query_span_width), packed_kv], 1
    )
    by_heads = lax.all_to_all(outgoing, "sp", split_axis=2, concat_axis=0, tiled=True)
    query_matrix = by_heads[:, 0].reshape(seq_len, local_key_value, 2, HEAD_SIZE)
    kv_pairs = by_heads[:, 1].reshape(seq_len, local_key_value, 2, HEAD_SIZE)
    key_rows = kv_pairs[:, :, 0]
    value_rows = kv_pairs[:, :, 1]
    segment_ids = segments[0]
    key_pos = jnp.arange(seq_len, dtype=jnp.int32)

    def block_scores(block_id):
        first_row = block_id * span
        query_rows = lax.dynamic_slice_in_dim(query_matrix, first_row, span, 0)
        row_pos = first_row + jnp.arange(span, dtype=jnp.int32)
        row_segments = lax.dynamic_slice_in_dim(segment_ids, first_row, span, 0)
        allowed = (key_pos[None, :] <= row_pos[:, None]) & (
            row_segments[:, None] == segment_ids[None, :]
        )
        scores = (
            jnp.einsum("igjd,kgd->gjik", query_rows, key_rows, preferred_element_type=jnp.float32)
            * score_scale
        )
        return (query_rows, jnp.where(allowed, scores, -jnp.inf))

    def attend(block_id):
        query_rows, scores = block_scores(block_id)
        row_top = jnp.max(scores, -1, keepdims=True)
        expo = jnp.exp(scores - row_top)
        row_total = jnp.sum(expo, -1, keepdims=True)
        probs = (expo / row_total).astype(jnp.bfloat16)
        context_rows = jnp.einsum(
            "gjik,kgd->igjd", probs, value_rows, preferred_element_type=jnp.float32
        )
        return (
            context_rows.astype(jnp.bfloat16).reshape(span, local_width),
            (row_top + jnp.log(row_total))[..., 0],
        )

    ctx_blocks, log_sums = lax.map(attend, jnp.arange(block_count, dtype=jnp.int32))
    context = lax.all_to_all(
        ctx_blocks.reshape(seq_len, local_width), "sp", split_axis=0, concat_axis=1, tiled=True
    )
    attended = jnp.dot(context, out_full, preferred_element_type=jnp.float32)
    middle = hidden_in + RESIDUAL * attended
    normed_two, norm_two_pull = jax.vjp(rms_norm, middle, gain_two.astype(jnp.float32))
    normed_two = normed_two.astype(jnp.bfloat16)
    logits = jnp.dot(normed_two, router_full, preferred_element_type=jnp.float32)

    def route(logit_rows):
        return jax.nn.softmax(jnp.take_along_axis(logit_rows, top_idx, 1), axis=-1)

    gate_prob, route_pull = jax.vjp(route, logits)
    expert_of, slot_rank = slot_table(top_idx)
    slot_index = expert_of * capacity + slot_rank
    inverse = (
        jnp.full((E * capacity,), -1, jnp.int32)
        .at[slot_index]
        .set(jnp.arange(count_of_rows * top_count, dtype=jnp.int32))
    )
    is_filled = (inverse >= 0)[:, None]
    pair_index = jnp.maximum(inverse, 0)
    routed = jnp.where(
        is_filled, normed_two[pair_index // top_count], jnp.zeros((), jnp.bfloat16)
    ).reshape(E, capacity, width)

    def from_owner(buffer):
        return lax.all_to_all(buffer, "sp", split_axis=1, concat_axis=0, tiled=True)

    def to_owner(buffer):
        return lax.all_to_all(buffer, "sp", split_axis=0, concat_axis=1, tiled=True)

    owner_rows = to_owner(routed)
    pre_act, activated, produced = expert_forward(owner_rows, experts_in, experts_out)
    returned = from_owner(produced)
    picked = (
        returned.reshape(E * capacity, width)[slot_index]
        .reshape(count_of_rows, top_count, width)
        .astype(jnp.float32)
    )
    mixed = jnp.einsum("tk,tkd->td", gate_prob, picked)
    block_out = middle + RESIDUAL * mixed
    grad_final = cotangent.astype(jnp.float32)
    grad_mixed = RESIDUAL * grad_final
    grad_gate = jnp.einsum("tkd,td->tk", picked, grad_mixed)
    (grad_logits,) = route_pull(grad_gate)
    grad_pairs = (
        (gate_prob[..., None] * grad_mixed[:, None, :])
        .astype(jnp.bfloat16)
        .reshape(count_of_rows * top_count, width)
    )
    grad_routed = jnp.where(is_filled, grad_pairs[pair_index], jnp.zeros((), jnp.bfloat16)).reshape(
        E, capacity, width
    )
    grad_owner = to_owner(grad_routed)
    grad_act = down_backward(grad_owner, experts_out)
    grad_rows, grad_pre = expert_backward(pre_act, experts_in, grad_act)
    grad_inner, grad_outer = weight_grads(owner_rows, activated, grad_pre, grad_owner)
    grad_back = from_owner(grad_rows)
    grad_inner, grad_outer = (
        lax.psum_scatter(
            grad_inner.astype(jnp.bfloat16), "fsdp", scatter_dimension=1, tiled=True
        ).astype(jnp.float32),
        lax.psum_scatter(
            grad_outer.astype(jnp.bfloat16), "fsdp", scatter_dimension=1, tiled=True
        ).astype(jnp.float32),
    )
    gathered_back = (
        grad_back.reshape(E * capacity, width)[slot_index]
        .reshape(count_of_rows, top_count, width)
        .astype(jnp.float32)
    )
    router_f32 = router_full.astype(jnp.float32)
    grad_normed_two = jnp.sum(gathered_back, 1) + jnp.dot(
        grad_logits, router_f32.T, precision=lax.Precision.HIGHEST
    )
    router_grad = jnp.dot(
        normed_two.astype(jnp.float32).T, grad_logits, precision=lax.Precision.HIGHEST
    )
    grad_middle_norm, gain_two_grad = norm_two_pull(grad_normed_two)
    grad_middle = grad_final + grad_middle_norm
    grad_attended = (RESIDUAL * grad_middle).astype(jnp.bfloat16)
    out_grad = jnp.einsum("tc,td->cd", context, grad_attended, preferred_element_type=jnp.float32)
    grad_context = jnp.einsum(
        "td,cd->tc", grad_attended, out_full, preferred_element_type=jnp.float32
    ).astype(jnp.bfloat16)
    context_heads = lax.all_to_all(
        grad_context, "sp", split_axis=1, concat_axis=0, tiled=True
    ).reshape(seq_len, local_key_value, 2, HEAD_SIZE)

    def attend_back(running, block_id):
        query_rows, scores = block_scores(block_id)
        probs = jnp.exp(scores - log_sums[block_id][..., None])
        grad_rows_blk = lax.dynamic_slice_in_dim(context_heads, block_id * span, span, 0)
        grad_probs = jnp.einsum(
            "igjd,kgd->gjik", grad_rows_blk, value_rows, preferred_element_type=jnp.float32
        )
        row_dot = jnp.sum(grad_probs * probs, -1, keepdims=True)
        grad_scores = (probs * (grad_probs - row_dot) * score_scale).astype(jnp.bfloat16)
        grad_query = jnp.einsum(
            "gjik,kgd->igjd", grad_scores, key_rows, preferred_element_type=jnp.float32
        )
        grad_key = running[0] + jnp.einsum(
            "gjik,igjd->kgd", grad_scores, query_rows, preferred_element_type=jnp.float32
        )
        grad_value = running[1] + jnp.einsum(
            "gjik,igjd->kgd",
            probs.astype(jnp.bfloat16),
            grad_rows_blk,
            preferred_element_type=jnp.float32,
        )
        return ((grad_key, grad_value), grad_query.astype(jnp.bfloat16).reshape(span, local_width))

    zero_kv = jnp.zeros((seq_len, local_key_value, HEAD_SIZE), jnp.float32)
    (grad_key, grad_value), grad_query = lax.scan(
        attend_back, (zero_kv, zero_kv), jnp.arange(block_count, dtype=jnp.int32)
    )
    grad_kv = (
        jnp.stack([grad_key, grad_value], 2).astype(jnp.bfloat16).reshape(seq_len, local_width)
    )
    outgoing_back = jnp.stack([grad_query.reshape(seq_len, local_width), grad_kv], 1)
    row_ordered = lax.all_to_all(outgoing_back, "sp", split_axis=0, concat_axis=2, tiled=True)
    grad_q_rows = row_ordered[:, 0].reshape(count_of_rows, HQ, HEAD_SIZE).astype(jnp.float32)
    key_value_gradient_rows = row_ordered[:, 1].reshape(
        count_of_rows, KEY_VALUE_HEADS, 2, HEAD_SIZE
    )
    grad_q_pre, grad_k_pre = rope_pull(
        (grad_q_rows, key_value_gradient_rows[:, :, 0].astype(jnp.float32))
    )
    grad_proj = jnp.concatenate(
        [
            grad_q_pre.reshape(count_of_rows, query_span_width),
            grad_k_pre.reshape(count_of_rows, key_span_width),
            key_value_gradient_rows[:, :, 1]
            .astype(jnp.float32)
            .reshape(count_of_rows, key_span_width),
        ],
        1,
    ).astype(jnp.bfloat16)
    qkv_grad = jnp.einsum("tc,tp->cp", normed_one, grad_proj, preferred_element_type=jnp.float32)
    grad_normed_one = jnp.einsum(
        "tp,cp->tc", grad_proj, qkv_full, preferred_element_type=jnp.float32
    )
    grad_hidden_norm, gain_one_grad = norm_one_pull(grad_normed_one)
    input_grad = grad_middle + grad_hidden_norm
    gain_one_grad, qkv_grad, out_grad, gain_two_grad, router_grad = (
        lax.psum_scatter(gain_one_grad, ("fsdp", "sp"), scatter_dimension=0, tiled=True),
        lax.psum_scatter(qkv_grad, ("fsdp", "sp"), scatter_dimension=0, tiled=True),
        lax.psum_scatter(out_grad, ("fsdp", "sp"), scatter_dimension=0, tiled=True),
        lax.psum_scatter(gain_two_grad, ("fsdp", "sp"), scatter_dimension=0, tiled=True),
        lax.psum_scatter(router_grad, ("fsdp", "sp"), scatter_dimension=0, tiled=True),
    )
    return (
        block_out,
        input_grad,
        gain_one_grad,
        qkv_grad,
        out_grad,
        gain_two_grad,
        router_grad,
        grad_inner,
        grad_outer,
    )


def solution(mesh):
    in_specs = (
        P(("fsdp", "sp"), None),
        P("fsdp", None),
        P(("fsdp", "sp"), None),
        P(("fsdp", "sp"), None),
        P(("fsdp", "sp")),
        P(("fsdp", "sp"), None),
        P(("fsdp", "sp"), None),
        P(("fsdp", "sp")),
        P(("fsdp", "sp"), None),
        P("sp", "fsdp", None),
        P("sp", "fsdp", None),
    )
    out_specs = (
        P(("fsdp", "sp"), None),
        P(("fsdp", "sp"), None),
        P(("fsdp", "sp")),
        P(("fsdp", "sp"), None),
        P(("fsdp", "sp"), None),
        P(("fsdp", "sp")),
        P(("fsdp", "sp"), None),
        P("sp", "fsdp", None),
        P("sp", "fsdp", None),
    )
    return jax.shard_map(shards, mesh=mesh, in_specs=in_specs, out_specs=out_specs, check_vma=False)
```

profile of v0, /device:TPU:1, one launch (start us, length us, event | category | flops | bytes accessed | tf_op | source)
XLA Modules:
  0.0 2033.0 jit_solution(12949885387280254634)
XLA Ops:
  12.8 69.5 %all-reduce.10 = (bf16[1024]{0:T(1024)(128)(2,1)S(1)}, bf16[1024]{0:T(1024)(128)(2,1)S(1)}) all-reduce(bf16[1024]{0:T(1024)(128)(2,1)S(1)} %dynamic-update-slice, bf16[1024]{0:T(1024)(128)(2,1)S(1)} %dynamic-update-slice.1), channel_id=1, replica_groups=mesh['fsdp'=16,'sp'=8] {'fsdp','sp'}, use_global_device_ids=true, to_apply=%add.4 | all-reduce | flops 2048 | bytes 8192
  83.5 4.5 reduce-window.6
  88.6 4.3 scatter_custom_fusion
  93.2 3.1 fusion.85
  97.2 1.3 copy.263
  98.5 4.4 all-to-all-start
  103.8 8.6 all-to-all-done
  113.9 12.6 while.28
  117.9 1.5 fusion.169
  124.2 1.5 fusion.169
  126.5 4.2 all-to-all-start.1
  130.7 34.2 %all_gather.25 = bf16[1024,16]{1,0:T(8,128)(2,1)S(1)} all-gather(bf16[8,16]{1,0:T(8,128)(2,1)S(1)} %copy-done.44), channel_id=1, replica_groups=mesh['fsdp'=16,'sp'=8] {'fsdp','sp'}, dimensions={0}, use_global_device_ids=true | all-gather | bytes 33024 | tf_op jit(solution)/shard_map/all_gather | solution.py:123
  165.4 2.3 multiply_reduce_fusion.2
  168.8 7.0 gather_fusion.4
  176.3 9.7 gather_fusion
  186.0 1.4 fusion.59
  187.4 9.6 gather_fusion.2
  196.9 5.1 broadcast_select_fusion
  202.1 53.2 %all_to_all.137 = bf16[16,128,1024]{2,1,0:T(8,128)(2,1)} all-to-all(bf16[16,128,1024]{2,1,0:T(8,128)(2,1)S(1)} %get-tuple-element.312), channel_id=1, replica_groups=mesh['fsdp'=16,'sp'=8] {'sp'}, dimensions={0} | all-to-all | bytes 8388608 | tf_op jit(solution)/shard_map/all_to_all | solution.py:229
  255.3 5.5 all-to-all-start.4
  261.3 4.8 copy.277
  266.1 43.5 %all-to-all-done.4 = bf16[16,128,1024]{2,1,0:T(8,128)(2,1)} async-done(((bf16[16,128,1024]{2,1,0:T(8,128)(2,1)}), bf16[16,128,1024]{2,1,0:T(8,128)(2,1)}, u32[]{:S(2)}, u32[]{:S(2)}) %all-to-all-start.4) | async-done | bytes 4194336 | tf_op jit(solution)/shard_map/all_to_all | solution.py:229
  309.7 4.7 copy.282
  314.4 11.3 fusion.119
  325.7 11.3 multiply_convert_fusion.1
  338.4 14.2 convolution_convert_fusion.1
  352.6 8.5 copy.279
  361.1 5.4 all-to-all-start.3
  367.0 48.5 %all-to-all-done.3 = bf16[2,1024,1024]{2,0,1:T(2,128)(2,1)} async-done(((bf16[2,1024,1024]{2,0,1:T(2,128)(2,1)}), bf16[2,1024,1024]{2,0,1:T(2,128)(2,1)}, u32[]{:S(2)}, u32[]{:S(2)}) %all-to-all-start.3) | async-done | bytes 4194336 | tf_op jit(solution)/shard_map/all_to_all | solution.py:226
  415.5 5.6 copy.280
  421.0 7.7 gather_fusion.1
  430.3 6.5 scatter_custom_fusion.1
  438.1 7.2 convolution_convert_fusion.2
  445.6 10.6 fusion.63
  456.2 8.6 fusion.62
  464.8 6.7 copy.284
  471.6 5.4 all-to-all-start.5
  477.8 48.7 %all-to-all-done.5 = bf16[2,1024,1024]{2,0,1:T(2,128)(2,1)} async-done(((bf16[2,1024,1024]{2,0,1:T(2,128)(2,1)}), bf16[2,1024,1024]{2,0,1:T(2,128)(2,1)}, u32[]{:S(2)}, u32[]{:S(2)}) %all-to-all-start.5) | async-done | bytes 4194336 | tf_op jit(solution)/shard_map/all_to_all | solution.py:226
  526.4 5.6 copy.285
  532.0 8.2 gather_fusion.3
  540.2 1.4 convert_reduce_fusion
  541.7 2.0 multiply_reduce_fusion
  547.1 4.2 all-to-all-start.6
  551.3 2.7 fusion.82
  554.2 3.5 all-to-all-done.6
  559.4 38.1 %while.29 = (s32[]{:T(128)}, f32[1024,1,64]{0,2,1:T(8,128)S(1)}, f32[1024,1,64]{0,2,1:T(8,128)}, bf16[2,512,128]{2,1,0:T(8,128)(2,1)}, s32[2]{0:T(128)}, /*index...) while((s32[]{:T(128)}, f32[1024,1,64]{0,2,1:T(8,128)S(1)}, ...), condition=%wide.region_18.19_spmd.clone, body=%wide.region_16.18_spmd.clone.sunk | while | flops 689765888 | bytes 55618452 | solution.py:313
  561.8 2.7 fusion.178
  566.5 3.9 fusion.180
  570.5 1.5 fusion.181
  574.0 4.3 fusion.183
  580.9 2.7 fusion.178
  585.5 3.9 fusion.180
  589.5 1.5 fusion.181
  593.1 4.4 fusion.183
  600.3 12.8 all_to_all.138
  614.0 4.7 fusion.79
  620.0 37.5 %reduce-scatter.11.cloned.1.call-done = bf16[2,64,512]{2,1,0:T(8,128)(2,1)} async-done(((bf16[2,1024,512]{2,1,0:T(8,128)(2,1)}), bf16[2,64,512]{2,1,0:T(8,128)(2,1)}) %reduce-scatter.11.cloned.1.call-update) | async-done | bytes 131088 | tf_op jit(solution)/shard_map/reduce_scatter | solution.py:262
  657.5 1.6 convert_element_type.187
  659.2 3.8 fusion.73
  663.0 66.5 %all-reduce.9 = (f32[1024]{0:T(1024)S(1)}, f32[1024]{0:T(1024)S(1)}) all-reduce(f32[1024]{0:T(1024)S(1)} %get-tuple-element.232, f32[1024]{0:T(1024)S(1)} %copy-done.37), channel_id=2, replica_groups=mesh['fsdp'=16,'sp'=8] {'fsdp','sp'}, use_global_device_ids=true, to_apply=%region_21.22.clone | all-reduce | flops 2048 | bytes 16384
  731.7 6.2 reduce-scatter.9.cloned.1.call-done
  737.9 1.8 convert_element_type.185
  739.6 639.8 %reduce-scatter.7.cloned.1.call-done = f32[8,1024]{1,0:T(8,128)} async-done(((f32[1024,1024]{1,0:T(8,128)}), f32[8,1024]{1,0:T(8,128)}) %reduce-scatter.7.cloned.1.call-update) | async-done | bytes 32784 | tf_op jit(solution)/shard_map/reduce_scatter | solution.py:347
  1379.5 646.8 %reduce-scatter.5.cloned.1.call-done = f32[8,2048]{1,0:T(8,128)} async-done(((f32[1024,2048]{1,0:T(8,128)}), f32[8,2048]{1,0:T(8,128)}) %reduce-scatter.5.cloned.1.call-update) | async-done | bytes 65552 | tf_op jit(solution)/shard_map/reduce_scatter | solution.py:346
  (288 shorter events, 47.1 us)
Async XLA Ops:
  7.2 86.0 %all-gather.5.cloned.1.call-start = ((), (), s32[]{:S(2)}) async-start(), calls=%async_computation.12 | async-start | bytes 4227072 | tf_op jit(solution)/shard_map/all_gather | solution.py:121
  7.9 157.5 %all-gather.7.cloned.1.call-start = ((), (), s32[]{:S(2)}) async-start(), calls=%async_computation.13 | async-start | bytes 2113536 | tf_op jit(solution)/shard_map/all_gather | solution.py:122
  8.7 305.8 %all-gather.9.cloned.1.call-start = ((), (), s32[]{:S(2)}) async-start(), calls=%async_computation.14 | async-start | bytes 4456448 | tf_op jit(solution)/shard_map/all_gather | solution.py:126
  82.3 14.0 copy-start.27
  83.4 4.8 copy-start.45
  83.4 12.9 copy-start.38
  96.4 6.5 copy-start.31
  96.4 6.5 copy-start.17
  97.2 16.7 copy-start.21
  98.5 13.9 all-to-all-start
  113.9 16.8 copy-start.44
  113.9 51.5 %copy-start.8 = (bf16[128,1024]{1,0:T(8,128)(2,1)S(1)}, bf16[128,1024]{1,0:T(8,128)(2,1)}, u32[]{:S(2)}) copy-start(bf16[128,1024]{1,0:T(8,128)(2,1)} %param.15) | copy-start | bytes 786436
  126.5 41.2 %copy-start.10 = (bf16[1024,1,64]{0,2,1:T(8,128)(2,1)}, bf16[1024,1,64]{0,2,1:T(8,128)(2,1)S(1)}, u32[]{:S(2)}) copy-start(bf16[1024,1,64]{0,2,1:T(8,128)(2,1)S(1)} %get-tuple-element.569) | copy-start | bytes 393220
  126.5 49.3 %copy-start.32 = (f32[2,1,2,512]{3,2,1,0:T(2,128)}, f32[2,1,2,512]{3,2,1,0:T(2,128)S(1)}, u32[]{:S(2)}) copy-start(f32[2,1,2,512]{3,2,1,0:T(2,128)S(1)} %get-tuple-element.505) | copy-start | bytes 24580
  126.5 38.6 %all-to-all-start.1 = ((bf16[8,128,128]{2,1,0:T(8,128)(2,1)}), bf16[8,128,128]{2,1,0:T(8,128)(2,1)S(1)}, u32[]{:S(2)}, u32[]{:S(2)}) async-start(bf16[8,128,128]{2,1,0:T(8,128)(2,1)} %bitcast.14), calls=%async_computation.1 | async-start | bytes 524288 | tf_op jit(solution)/shard_map/all_to_all | solution.py:199
  164.9 10.9 copy-start.15
  164.9 10.9 copy-start.29
  165.3 10.5 copy-start.19
  167.7 8.2 copy-start.49
  167.7 8.2 copy-start.42
  176.1 254.0 %copy-start.35 = (f32[128]{0:T(128)}, f32[128]{0:T(128)S(1)}, u32[]{:S(2)}) copy-start(f32[128]{0:T(128)S(1)} %get-tuple-element.280) | copy-start | bytes 1540
  176.1 254.0 %copy-start.40 = (f32[128]{0:T(128)}, f32[128]{0:T(128)S(1)}, u32[]{:S(2)}) copy-start(f32[128]{0:T(128)S(1)} %fusion.106) | copy-start | bytes 1540
  255.3 54.4 %all-to-all-start.4 = ((bf16[16,128,1024]{2,1,0:T(8,128)(2,1)}), bf16[16,128,1024]{2,1,0:T(8,128)(2,1)}, u32[]{:S(2)}, u32[]{:S(2)}) async-start(bf16[16,128,1024]{2,1,0:T(8,128)(2,1)} %get-tuple-element.311), calls=%async_computation.4 | async-start | bytes 8388608 | tf_op jit(solution)/shard_map/all_to_all | solution.py:229
  260.8 64.9 %all-gather.11.cloned.1.call-start = ((), (), s32[]{:S(2)}) async-start(), calls=%async_computation.15 | async-start | bytes 2228224 | tf_op jit(solution)/shard_map/all_gather | solution.py:127
  325.7 12.7 copy-start.51
  361.1 5.4 copy-start.48
  361.1 5.5 copy-start.47
  361.1 54.4 %all-to-all-start.3 = ((bf16[2,1024,1024]{2,0,1:T(2,128)(2,1)}), bf16[2,1024,1024]{2,0,1:T(2,128)(2,1)}, u32[]{:S(2)}, u32[]{:S(2)}) async-start(bf16[2,1024,1024]{2,0,1:T(2,128)(2,1)} %copy.279), calls=%async_computation.3 | async-start | bytes 8388608 | tf_op jit(solution)/shard_map/all_to_all | solution.py:226
  366.5 252.2 %all-reduce.13.cloned.1.call-start = ((), (), s32[]{:S(2)}) async-start(), calls=%async_computation.20 | async-start | bytes 1048576
  366.9 54.1 %copy-start.34 = (s32[1024]{0:T(1024)}, s32[1024]{0:T(1024)S(1)}, u32[]{:S(2)}) copy-start(s32[1024]{0:T(1024)S(1)} %broadcast_clamp_fusion) | copy-start | bytes 12292
  428.7 16.6 copy-start.1
  438.1 219.5 %reduce-scatter.11.cloned.1.call-start = ((), (), s32[]{:S(2)}) async-start(), calls=%async_computation.19 | async-start | bytes 2228224 | tf_op jit(solution)/shard_map/reduce_scatter | solution.py:262
  445.3 292.5 %reduce-scatter.9.cloned.1.call-start = ((), (), s32[]{:S(2)}) async-start(), calls=%async_computation.18 | async-start | bytes 4456448 | tf_op jit(solution)/shard_map/reduce_scatter | solution.py:259
  471.6 5.4 copy-start.36
  471.6 5.4 copy-start.41
  471.6 54.9 %all-to-all-start.5 = ((bf16[2,1024,1024]{2,0,1:T(2,128)(2,1)}), bf16[2,1024,1024]{2,0,1:T(2,128)(2,1)}, u32[]{:S(2)}, u32[]{:S(2)}) async-start(bf16[2,1024,1024]{2,0,1:T(2,128)(2,1)} %copy.284), calls=%async_computation.5 | async-start | bytes 8388608 | tf_op jit(solution)/shard_map/all_to_all | solution.py:226
  532.0 9.7 copy-start.7
  532.0 9.7 copy-start.16
  532.0 9.7 copy-start.30
  540.2 4.2 copy-start.18
  540.2 4.2 copy-start.43
  543.8 7.5 copy-start.20
  545.5 8.5 copy-start.4
  547.1 10.7 all-to-all-start.6
  551.3 8.1 copy-start.11
  551.3 8.1 copy-start.33
  551.3 828.2 %reduce-scatter.7.cloned.1.call-start = ((), (), s32[]{:S(2)}) async-start(), calls=%async_computation.17 | async-start | bytes 4227072 | tf_op jit(solution)/shard_map/reduce_scatter | solution.py:347
  554.0 1472.3 %reduce-scatter.5.cloned.1.call-start = ((), (), s32[]{:S(2)}) async-start(), calls=%async_computation.16 | async-start | bytes 8454144 | tf_op jit(solution)/shard_map/reduce_scatter | solution.py:346
  559.4 11.1 copy-start.13
  566.5 4.0 copy-start
  573.5 4.8 copy-start.12
  574.0 4.3 copy-start.14
  578.3 11.1 copy-start.13
  585.5 4.0 copy-start
  592.5 5.0 copy-start.12
  593.1 4.4 copy-start.14
  597.5 16.2 copy-start.23
  597.5 16.2 copy-start.25
  599.7 14.2 copy-start.9
  599.7 14.2 copy-start.28
  599.7 14.2 copy-start.39
  618.7 44.3 %copy-start.37 = (f32[1024]{0:T(1024)S(1)}, f32[1024]{0:T(1024)}, u32[]{:S(2)}) copy-start(f32[1024]{0:T(1024)} %get-tuple-element.230) | copy-start | bytes 12292
  618.7 112.0 %copy-start.46 = (f32[128]{0:T(128)S(1)}, f32[128]{0:T(128)}, u32[]{:S(2)}) copy-start(f32[128]{0:T(128)} %copy-done.45) | copy-start | bytes 1540
  618.7 112.0 %copy-start.5 = (f32[128,1024]{1,0:T(8,128)S(1)}, f32[128,1024]{1,0:T(8,128)}, u32[]{:S(2)}) copy-start(f32[128,1024]{1,0:T(8,128)} %copy-done.4) | copy-start | bytes 1572868
  (8 other events, 24.3 us)
Sparse Core Ops, SparseCore 0:
  11.2 70.5 all-gather.4
  85.0 62.9 all-gather.6
  150.1 48.4 all-gather.8
  263.4 42.2 all-gather.10
  438.2 144.6 all-reduce.12
  586.4 71.1 reduce-scatter.10
  660.9 76.9 reduce-scatter.8
  740.9 638.5 reduce-scatter.6
  1382.4 643.8 reduce-scatter.4
where the time goes:
time: 2050 us; the launch traced here: 2030 us
  waiting for transfers between devices  1490 us (73%)
  blocking collectives  236 us (12%)
  matrix products  116 us (6%)
  local copies, waits for them, and re-layouts  106 us (5%)
  other arithmetic  37.5 us (2%)
  starting transfers between devices  29.7 us (1%)
    reduce_scatter x1, waiting for transfers between devices, shards(): lax.psum_scatter(qkv_grad, ('fsdp', 'sp'), scatter_dimension=0, tiled=True)  647 us
    reduce_scatter x1, waiting for transfers between devices, shards(): lax.psum_scatter(out_grad, ('fsdp', 'sp'), scatter_dimension=0, tiled=True)  640 us
    unnamed x2, blocking collectives  136 us
    all_to_all x2, waiting for transfers between devices, from_owner(): return lax.all_to_all(buffer, 'sp', split_axis=1, concat_axis=0, tiled=True)  97.1 us
    all_to_all x1, blocking collectives, to_owner(): return lax.all_to_all(buffer, 'sp', split_axis=0, concat_axis=1, tiled=True)  53.2 us
    all_to_all x1, waiting for transfers between devices, to_owner(): return lax.all_to_all(buffer, 'sp', split_axis=0, concat_axis=1, tiled=True)  43.5 us
  transfers between devices with their start and end apart: 15, of which 9 were waited for; matrix products, arithmetic and copies ran while one was open for 10% of the time, Pallas kernels for 0%

commit v1 on v0

v1 whole, which is shorter than its diff:
```python
import jax
import jax.numpy as jnp
import numpy as np
from jax import lax
from jax.sharding import PartitionSpec as P

HQ = 16
KEY_VALUE_HEADS = 8
HEAD_SIZE = 64
E = 16
EPSILON = 1e-06
RESIDUAL = 0.22
BLOCK = 256
LONGEST = 512
BF16 = jnp.bfloat16
F32 = jnp.float32


def rope_tables(count):
    frequency = np.float32(10000.0) ** (
        np.float32(-2.0) * np.arange(HEAD_SIZE // 2, dtype=np.float32) / np.float32(HEAD_SIZE)
    )
    angles = np.arange(count, dtype=np.float32)[:, None] * frequency.astype(np.float32)[None, :]
    cosine = np.cos(angles).astype(np.float32)
    sine = np.sin(angles).astype(np.float32)
    return np.concatenate([cosine, cosine], 1), np.concatenate([-sine, sine], 1)


def swap_halves(value):
    half = HEAD_SIZE // 2
    return jnp.concatenate([value[..., half:], value[..., :half]], -1)


def dot(left, right, contract):
    return lax.dot_general(left, right, (contract, ((), ())), preferred_element_type=F32)


def inverse_rms(value):
    return lax.rsqrt(jnp.mean(value * value, -1, keepdims=True) + EPSILON)


def rms_backward(grad, value, inverse, gain):
    scaled = grad * gain
    return inverse * scaled - value * (inverse**3) * jnp.mean(scaled * value, -1, keepdims=True)


def block_keys(block, seq_len):
    return max(0, block * BLOCK - LONGEST), (block + 1) * BLOCK


def allowed_pairs(segment_ids, row_lo, row_hi, key_lo, key_hi):
    rows = row_lo + jnp.arange(row_hi - row_lo, dtype=jnp.int32)
    keys = key_lo + jnp.arange(key_hi - key_lo, dtype=jnp.int32)
    return (keys[None, :] <= rows[:, None]) & (
        segment_ids[row_lo:row_hi, None] == segment_ids[None, key_lo:key_hi]
    )


def attention_forward(query, key, value, segment_ids):
    seq_len = key.shape[0]
    scale = HEAD_SIZE**-0.5
    contexts, sums = [], []
    for block in range(seq_len // BLOCK):
        lo, hi = block * BLOCK, (block + 1) * BLOCK
        k_lo, k_hi = block_keys(block, seq_len)
        allowed = allowed_pairs(segment_ids, lo, hi, k_lo, k_hi)
        scores = (
            jnp.einsum("jid,kd->jik", query[:, lo:hi], key[k_lo:k_hi], preferred_element_type=F32)
            * scale
        )
        scores = jnp.where(allowed, scores, -jnp.inf)
        top = jnp.max(scores, -1, keepdims=True)
        expo = jnp.exp(scores - top)
        total = jnp.sum(expo, -1, keepdims=True)
        probs = (expo / total).astype(BF16)
        contexts.append(
            jnp.einsum("jik,kd->ijd", probs, value[k_lo:k_hi], preferred_element_type=F32)
            .astype(BF16)
            .reshape(BLOCK, 2 * HEAD_SIZE)
        )
        sums.append(top + jnp.log(total))
    return jnp.concatenate(contexts, 0), sums


def attention_backward(query, key, value, segment_ids, sums, grad_context):
    seq_len = key.shape[0]
    scale = HEAD_SIZE**-0.5
    grad_heads = grad_context.reshape(seq_len, 2, HEAD_SIZE).transpose(1, 0, 2)
    grad_query = []
    grad_key = [0.0] * (seq_len // BLOCK)
    grad_value = [0.0] * (seq_len // BLOCK)
    for block in range(seq_len // BLOCK):
        lo, hi = block * BLOCK, (block + 1) * BLOCK
        k_lo, k_hi = block_keys(block, seq_len)
        allowed = allowed_pairs(segment_ids, lo, hi, k_lo, k_hi)
        keys, values = key[k_lo:k_hi], value[k_lo:k_hi]
        scores = (
            jnp.einsum("jid,kd->jik", query[:, lo:hi], keys, preferred_element_type=F32) * scale
        )
        probs = jnp.exp(jnp.where(allowed, scores, -jnp.inf) - sums[block])
        grad_rows = grad_heads[:, lo:hi]
        grad_probs = jnp.einsum("jid,kd->jik", grad_rows, values, preferred_element_type=F32)
        row_dot = jnp.sum(grad_probs * probs, -1, keepdims=True)
        grad_scores = (probs * (grad_probs - row_dot) * scale).astype(BF16)
        grad_query.append(
            jnp.einsum("jik,kd->jid", grad_scores, keys, preferred_element_type=F32)
        )
        new_key = jnp.einsum(
            "jik,jid->kd", grad_scores, query[:, lo:hi], preferred_element_type=F32
        )
        new_value = jnp.einsum(
            "jik,jid->kd", probs.astype(BF16), grad_rows, preferred_element_type=F32
        )
        for piece in range(k_lo // BLOCK, k_hi // BLOCK):
            at = piece * BLOCK - k_lo
            grad_key[piece] = grad_key[piece] + new_key[at : at + BLOCK]
            grad_value[piece] = grad_value[piece] + new_value[at : at + BLOCK]
    return (
        jnp.concatenate(grad_query, 1).astype(BF16),
        jnp.concatenate(grad_key, 0).astype(BF16),
        jnp.concatenate(grad_value, 0).astype(BF16),
    )


def shards(
    tokens,
    segments,
    top_idx,
    cotangent,
    norm1_gain,
    qkv_weight,
    out_weight,
    norm2_gain,
    router_weight,
    expert_in,
    expert_out,
):
    n_sp = lax.axis_size("sp")
    n_fsdp = lax.axis_size("fsdp")
    sp_index = lax.axis_index("sp")
    rows, width = tokens.shape
    seq_len = rows * n_sp
    weight_rows = qkv_weight.shape[0]
    hidden = expert_out.shape[2]
    q_span, k_span = HQ * HEAD_SIZE, KEY_VALUE_HEADS * HEAD_SIZE
    group = q_span // n_sp
    head = k_span // n_sp
    segment_ids = segments[0]

    def own(array):
        return lax.dynamic_slice_in_dim(array, sp_index * rows, rows, 0)

    def sum_over(array, axis, count):
        parts = lax.all_to_all(array, axis, split_axis=0, concat_axis=0, tiled=True)
        return jnp.sum(parts.astype(F32), 0)

    small = jnp.concatenate([norm1_gain[:, None], norm2_gain[:, None], router_weight], 1)
    small = jnp.pad(small, ((0, 0), (0, 128 - small.shape[1])))
    packed = jnp.concatenate(
        [
            qkv_weight[:, :q_span].reshape(weight_rows, n_sp, group),
            qkv_weight[:, q_span : q_span + k_span].reshape(weight_rows, n_sp, head),
            qkv_weight[:, q_span + k_span :].reshape(weight_rows, n_sp, head),
            jnp.broadcast_to(small[:, None], (weight_rows, n_sp, 128)),
        ],
        2,
    ).transpose(1, 0, 2)
    packed = lax.all_to_all(packed, "sp", split_axis=0, concat_axis=0, tiled=True)
    packed = lax.all_gather(
        packed.reshape(n_sp * weight_rows, packed.shape[2]), "fsdp", axis=0, tiled=True
    )
    tokens_all = lax.all_gather(tokens, "sp", axis=0, tiled=True)
    chosen = jnp.sum(
        (top_idx[:, :, None] == jnp.arange(128, dtype=jnp.int32)).astype(F32), 1
    ).astype(BF16)
    late = lax.all_gather(jnp.concatenate([cotangent, chosen], 1), "sp", axis=0, tiled=True)
    out_full = lax.all_gather(out_weight, ("fsdp", "sp"), axis=0, tiled=True)
    experts_in = lax.all_gather(expert_in, "fsdp", axis=1, tiled=True)
    experts_out = lax.all_gather(expert_out, "fsdp", axis=1, tiled=True)

    qkv_own = packed[:, : 2 * group]
    small_all = packed[:, 2 * group :].astype(F32).T
    gain_one, gain_two = small_all[0:1], small_all[1:2]
    router = packed[:, 2 * group + 2 : 2 * group + 2 + E]

    hidden_in = tokens_all.astype(F32)
    inverse_one = inverse_rms(hidden_in)
    normed_one = (hidden_in * inverse_one * gain_one).astype(BF16)
    projected = dot(normed_one, qkv_own, ((1,), (0,)))
    cosine, sine = rope_tables(seq_len)

    def rotate(value):
        return value * cosine + swap_halves(value) * sine

    def rotate_back(value):
        return value * cosine - swap_halves(value) * sine

    query = jnp.stack(
        [rotate(projected[:, :head]), rotate(projected[:, head:group])], 0
    ).astype(BF16)
    key = rotate(projected[:, group : group + head]).astype(BF16)
    value = projected[:, group + head :].astype(BF16)
    context, sums = attention_forward(query, key, value, segment_ids)
    contexts = lax.all_gather(context, "sp", axis=0, tiled=False)
    context_all = contexts.transpose(1, 0, 2).reshape(seq_len, width)
    attended = dot(context_all, out_full, ((1,), (0,)))
    middle = hidden_in + RESIDUAL * attended
    inverse_two = inverse_rms(middle)
    normed_two = (middle * inverse_two * gain_two).astype(BF16)
    logits = dot(normed_two, router, ((1,), (0,)))
    mask = late[:, width : width + E] > 0
    shown = jnp.where(mask, logits, -jnp.inf)
    expo = jnp.exp(shown - jnp.max(shown, -1, keepdims=True))
    gates = expo / jnp.sum(expo, -1, keepdims=True)
    grad_mixed = RESIDUAL * late[:, :width].astype(F32)

    mixed = 0.0
    grad_sum = 0.0
    extra = 0.0
    weight_sums = []
    lane = jnp.arange(128, dtype=jnp.int32)
    for local in range(expert_in.shape[0]):
        expert = sp_index * expert_in.shape[0] + local
        gate = jnp.sum(
            jnp.where(jnp.arange(E, dtype=jnp.int32) == expert, gates, 0.0), -1, keepdims=True
        )
        w_in, w_out = experts_in[local], experts_out[local]
        pre_act = dot(normed_two, w_in, ((1,), (0,)))
        gate_part, up_part = pre_act[:, :hidden], pre_act[:, hidden:]
        sigmoid = jax.nn.sigmoid(gate_part)
        activated = (gate_part * sigmoid * up_part).astype(BF16)
        produced = dot(activated, w_out, ((1,), (1,))).astype(BF16).astype(F32)
        mixed = mixed + gate * produced
        grad_gate = jnp.sum(grad_mixed * produced, -1, keepdims=True)
        extra = extra + jnp.where(lane == expert, gate * grad_gate, 0.0)
        grad_result = (gate * grad_mixed).astype(BF16)
        grad_act = dot(grad_result, w_out, ((1,), (0,)))
        grad_pre = jnp.concatenate(
            [
                grad_act * up_part * sigmoid * (1.0 + gate_part * (1.0 - sigmoid)),
                grad_act * gate_part * sigmoid,
            ],
            1,
        ).astype(BF16)
        grad_sum = grad_sum + dot(grad_pre, w_in, ((1,), (1,)))
        grad_in = dot(normed_two, grad_pre, ((0,), (0,))).astype(BF16)
        grad_out = dot(grad_result, activated, ((0,), (0,))).astype(BF16)
        weight_sums.append((grad_in, grad_out))

    mixed_own = lax.psum_scatter(mixed.astype(BF16), "sp", scatter_dimension=0, tiled=True)
    block_out = own(middle) + RESIDUAL * mixed_own.astype(F32)

    back = jnp.concatenate([grad_sum, extra], 1).astype(BF16)
    back = sum_over(back.reshape(n_sp, rows, width + 128), "sp", n_sp)
    weighted = back[:, width : width + E]
    gates_own, normed_own = own(gates), own(normed_two)
    grad_logits = weighted - gates_own * jnp.sum(weighted, -1, keepdims=True)
    grad_normed_two = back[:, :width] + lax.dot_general(
        grad_logits, router.astype(F32), (((1,), (1,)), ((), ())), precision=lax.Precision.HIGHEST
    )
    router_part = lax.dot_general(
        normed_own.astype(F32), grad_logits, (((0,), (0,)), ((), ())), precision=lax.Precision.HIGHEST
    )
    middle_own, inverse_own = own(middle), own(inverse_two)
    gain_two_part = jnp.sum(grad_normed_two * middle_own * inverse_own, 0)
    grad_middle = cotangent.astype(F32) + rms_backward(
        grad_normed_two, middle_own, inverse_own, gain_two
    )
    grad_attended = (RESIDUAL * grad_middle).astype(BF16)

    grad_attended_all = lax.all_gather(grad_attended, "sp", axis=0, tiled=True)
    grad_inner, grad_outer = [], []
    for grad_in, grad_out in weight_sums:
        grad_inner.append(sum_over(grad_in.reshape(n_fsdp, -1, width), "fsdp", n_fsdp))
        grad_outer.append(sum_over(grad_out.reshape(n_fsdp, -1, hidden), "fsdp", n_fsdp))

    out_own = lax.dynamic_slice_in_dim(out_full, sp_index * group, group, 0)
    grad_context = dot(grad_attended_all, out_own, ((1,), (1,))).astype(BF16)
    out_part = dot(context, grad_attended_all, ((0,), (0,)))
    out_sum = sum_over(
        out_part.astype(BF16).reshape(n_fsdp, group // n_fsdp, width), "fsdp", n_fsdp
    )
    shares = out_part.shape[0] // n_fsdp
    moves = []
    for f in range(n_fsdp):
        for s in range(n_sp):
            moves.append((f * n_sp + s, (s * group + f * shares) // weight_rows))
    if shares == weight_rows:
        out_grad = lax.ppermute(out_sum, ("fsdp", "sp"), moves)
    else:
        whole = lax.all_gather(out_sum, ("fsdp", "sp"), axis=0, tiled=False)
        whole = whole.reshape(n_fsdp, n_sp, shares, width).transpose(1, 0, 2, 3)
        device = lax.axis_index("fsdp") * n_sp + sp_index
        out_grad = lax.dynamic_slice_in_dim(
            whole.reshape(width, width), device * weight_rows, weight_rows, 0
        )

    grad_query, grad_key, grad_value = attention_backward(
        query, key, value, segment_ids, sums, grad_context
    )
    grad_proj = jnp.concatenate(
        [
            rotate_back(grad_query[0].astype(F32)),
            rotate_back(grad_query[1].astype(F32)),
            rotate_back(grad_key.astype(F32)),
            grad_value.astype(F32),
        ],
        1,
    ).astype(BF16)
    grad_first = dot(grad_proj, qkv_own, ((1,), (1,))).astype(BF16)
    grad_normed_one = sum_over(grad_first.reshape(n_sp, rows, width), "sp", n_sp)
    qkv_part = dot(normed_one, grad_proj, ((0,), (0,)))
    small_part = jnp.concatenate([gain_two_part[:, None], router_part], 1)
    small_part = jnp.pad(small_part, ((0, 0), (0, 128 - small_part.shape[1])))
    bundle = jnp.concatenate([qkv_part, small_part], 1).astype(BF16)
    bundle = sum_over(bundle.reshape(n_fsdp, -1, bundle.shape[1]), "fsdp", n_fsdp)
    bundle = lax.all_to_all(
        bundle.reshape(n_sp, weight_rows, bundle.shape[1]),
        "sp",
        split_axis=0,
        concat_axis=0,
        tiled=True,
    )
    qkv_grad = jnp.concatenate(
        [
            bundle[:, :, :group].transpose(1, 0, 2).reshape(weight_rows, q_span),
            bundle[:, :, group : group + head].transpose(1, 0, 2).reshape(weight_rows, k_span),
            bundle[:, :, group + head : 2 * group].transpose(1, 0, 2).reshape(weight_rows, k_span),
        ],
        1,
    )
    smalls = jnp.sum(bundle[:, :, 2 * group :], 0)
    gain_two_grad = smalls[:, 0]
    router_grad = smalls[:, 1 : 1 + E]
    gain_one_grad = jnp.sum(qkv_grad * qkv_weight.astype(F32), 1) / norm1_gain.astype(F32)
    hidden_own = tokens.astype(F32)
    input_grad = grad_middle + rms_backward(
        grad_normed_one, hidden_own, inverse_rms(hidden_own), gain_one
    )
    return (
        block_out,
        input_grad,
        gain_one_grad,
        qkv_grad,
        out_grad,
        gain_two_grad,
        router_grad,
        jnp.stack(grad_inner, 0),
        jnp.stack(grad_outer, 0),
    )


def solution(mesh):
    both = P(("fsdp", "sp"), None)
    flat = P(("fsdp", "sp"))
    expert = P("sp", "fsdp", None)
    return jax.shard_map(
        shards,
        mesh=mesh,
        in_specs=(both, P("fsdp", None), both, both, flat, both, both, flat, both, expert, expert),
        out_specs=(both, both, flat, both, both, flat, both, expert, expert),
        check_vma=False,
    )
```

time: 2050 us -> 593 us (0.29)
  the two profiles are of different devices: /device:TPU:1 before, /device:TPU:19 now
where the time goes in v1:
time: 593 us; the launch traced here: 584 us
  waiting for transfers between devices  272 us (46%)
  matrix products  119 us (20%)
  starting transfers between devices  70.2 us (12%)
  local copies, waits for them, and re-layouts  45.2 us (8%)
  other arithmetic  42.9 us (7%)
  blocking collectives  19.3 us (3%)
  between operations  15.9 us (3%)
    all_gather x1, waiting for transfers between devices, shards(): out_full = lax.all_gather(out_weight, ('fsdp', 'sp'), axis=0, tiled=True)  62.6 us
    dot_general x19, matrix products, dot(): lax.dot_general(left, right, (contract, ((), ())), preferred_element_type...  60.6 us
    all_to_all x8, waiting for transfers between devices, sum_over(): parts = lax.all_to_all(array, axis, split_axis=0, concat_axis=0, tiled=True)  55.4 us
    all_to_all x8, starting transfers between devices, sum_over(): parts = lax.all_to_all(array, axis, split_axis=0, concat_axis=0, tiled=True)  51.6 us
    all_gather x1, waiting for transfers between devices, shards(): experts_in = lax.all_gather(expert_in, 'fsdp', axis=1, tiled=True)  50.5 us
    all_gather x1, waiting for transfers between devices, shards(): experts_out = lax.all_gather(expert_out, 'fsdp', axis=1, tiled=True)  34.6 us
    all_gather x1, waiting for transfers between devices, shards(): contexts = lax.all_gather(context, 'sp', axis=0, tiled=False)  25.2 us
    all_gather x1, waiting for transfers between devices, shards(): lax.all_gather(jnp.concatenate([cotangent, chosen], 1), 'sp', axis=0, til...  23 us
  transfers between devices with their start and end apart: 19, of which 12 were waited for; matrix products, arithmetic and copies ran while one was open for 26% of the time, Pallas kernels for 0%

profile of v1, /device:TPU:19, one launch (start us, length us, event | category | flops | bytes accessed | tf_op | source)
XLA Modules:
  0.0 584.4 jit_solution(5444076086937399332)
XLA Ops:
  7.2 1.8 copy.130
  13.6 6.0 %all-to-all-start = ((bf16[8,8,384]{2,1,0:T(8,128)(2,1)}), bf16[8,8,384]{2,1,0:T(8,128)(2,1)S(1)}, u32[]{:S(2)}, u32[]{:S(2)}) async-start(bf16[8,8,384]{2,1,0:T(8,128)(2,1)} %maximum_bitcast_fusion), calls=%async_computation | async-start | bytes 98304 | tf_op jit(solution)/shard_map/all_to_all | solution.py:168
  22.5 1.9 all-to-all-done
  24.4 19.3 %all_gather.28 = bf16[1024,384]{1,0:T(8,128)(2,1)S(1)} all-gather(bf16[64,384]{1,0:T(8,128)(2,1)S(1)} %bitcast.210), channel_id=1, replica_groups=mesh['fsdp'=16,'sp'=8] {'fsdp'}, dimensions={0}, use_global_device_ids=true | all-gather | bytes 835584 | tf_op jit(solution)/shard_map/all_gather | solution.py:169
  44.3 2.2 fusion.8
  58.1 25.2 %all-gather.21.cloned.1.call-done = bf16[8192,128]{1,0:T(8,128)(2,1)} async-done(((bf16[1024,128]{1,0:T(8,128)(2,1)}), bf16[8192,128]{1,0:T(8,128)(2,1)}) %all-gather.21.cloned.1.call-update) | async-done | bytes 2097168 | tf_op jit(solution)/shard_map/all_gather | solution.py:204
  83.3 4.1 copy.140
  87.4 62.6 %all-gather.11.cloned.1.call-done = bf16[1024,1024]{1,0:T(8,128)(2,1)} async-done(((bf16[8,1024]{1,0:T(8,128)(2,1)}), bf16[1024,1024]{1,0:T(8,128)(2,1)}) %all-gather.11.cloned.1.call-update) | async-done | bytes 2097168 | tf_op jit(solution)/shard_map/all_gather | solution.py:177
  150.0 4.9 multiply_reduce_fusion
  155.0 1.9 copy-done.1
  157.3 23.0 %all-gather.13.cloned.1.call-done = bf16[1024,1152]{0,1:T(8,128)(2,1)} async-done(((bf16[128,1152]{0,1:T(8,128)(2,1)}), bf16[1024,1152]{0,1:T(8,128)(2,1)}) %all-gather.13.cloned.1.call-update) | async-done | bytes 2359312 | tf_op jit(solution)/shard_map/all_gather | solution.py:176
  182.5 50.5 %all-gather.15.cloned.1.call-done = bf16[2,1024,1024]{2,1,0:T(8,128)(2,1)} async-done(((bf16[2,64,1024]{2,1,0:T(8,128)(2,1)}), bf16[2,1024,1024]{2,1,0:T(8,128)(2,1)}) %all-gather.15.cloned.1.call-update) | async-done | bytes 4194320 | tf_op jit(solution)/shard_map/all_gather | solution.py:178
  233.0 6.1 %fusion.14 = f32[1024,1024]{0,1:T(8,128)} fusion(bf16[1024,1024]{0,1:T(8,128)(2,1)S(1)} %multiply_convert_fusion, bf16[2,1024,1024]{2,1,0:T(8,128)(2,1)} %all-gather.15.cloned.1.call-done), kind=kOutput, calls=%fused_computation.51 | convolution fusion | flops 2147483648 | bytes 8388608 | tf_op jit(solution)/shard_map/dot_general | solution.py:35
  239.1 4.4 fusion.15
  243.5 34.6 %all-gather.17.cloned.1.call-done = bf16[2,1024,512]{2,1,0:T(8,128)(2,1)} async-done(((bf16[2,64,512]{2,1,0:T(8,128)(2,1)}), bf16[2,1024,512]{2,1,0:T(8,128)(2,1)}) %all-gather.17.cloned.1.call-update) | async-done | bytes 2097168 | tf_op jit(solution)/shard_map/all_gather | solution.py:179
  278.1 5.4 multiply_convert_fusion.2
  287.6 2.4 multiply_convert_fusion.4
  290.1 3.1 fusion.6
  294.1 2.4 fusion.13
  296.5 2.4 add_convert_fusion
  298.9 1.7 pad_maximum_fusion
  300.7 5.9 %all-to-all-start.1 = ((bf16[8,128,1152]{2,1,0:T(8,128)(2,1)}), bf16[8,128,1152]{2,1,0:T(8,128)(2,1)}, u32[]{:S(2)}, u32[]{:S(2)}) async-start(bf16[8,128,1152]{2,1,0:T(8,128)(2,1)} %pad_maximum_fusion), calls=%async_computation.1 | async-start | bytes 4718592 | tf_op jit(solution)/shard_map/all_to_all | solution.py:154
  307.2 28.7 %all-to-all-done.1 = bf16[8,128,1152]{2,1,0:T(8,128)(2,1)} async-done(((bf16[8,128,1152]{2,1,0:T(8,128)(2,1)}), bf16[8,128,1152]{2,1,0:T(8,128)(2,1)}, u32[]{:S(2)}, u32[]{:S(2)}) %all-to-all-start.1) | async-done | bytes 2359328 | tf_op jit(solution)/shard_map/all_to_all | solution.py:154
  335.8 2.1 convert_reduce_fusion
  341.0 2.4 multiply_reduce_fusion.5
  343.9 2.0 multiply_convert_fusion.9
  350.9 4.1 fusion.42
  355.0 6.6 %all-to-all-start.8 = ((bf16[16,64,512]{2,1,0:T(8,128)(2,1)}), bf16[16,64,512]{2,1,0:T(8,128)(2,1)}, u32[]{:S(2)}, u32[]{:S(2)}) async-start(bf16[16,64,512]{2,1,0:T(8,128)(2,1)} %bitcast.202), calls=%async_computation.8 | async-start | bytes 2097152 | tf_op jit(solution)/shard_map/all_to_all | solution.py:154
  361.7 4.2 copy.163
  365.9 5.5 convolution_convert_fusion.3
  371.5 3.8 convolution_convert_fusion.2
  375.3 4.1 fusion.45
  381.5 2.1 convolution_convert_fusion.6
  386.5 6.8 %all-to-all-start.9 = ((bf16[16,64,512]{2,1,0:T(8,128)(2,1)}), bf16[16,64,512]{2,1,0:T(8,128)(2,1)S(1)}, u32[]{:S(2)}, u32[]{:S(2)}) async-start(bf16[16,64,512]{2,1,0:T(8,128)(2,1)} %bitcast.203), calls=%async_computation.9 | async-start | bytes 2097152 | tf_op jit(solution)/shard_map/all_to_all | solution.py:154
  393.3 6.3 %fusion.61 = f32[768,64]{0,1:T(8,128)} fusion(bf16[2,256,64]{1,2,0:T(8,128)(2,1)S(1)} %copy-done.42, f32[2,256,768]{2,1,0:T(8,128)} %fusion.164, f32[2,256,768]{2,1,0:T(8,128)} %copy-done.4, f32[2,256]{1,0:T(2,128)S(1)} %copy-done.65), kind=kOutput, calls=%fused_computation.99 | convolution fusion | flops 53085440 | bytes 3409920 | tf_op jit(solution)/shard_map/jik,jid->kd/dot_general | solution.py:108
  401.1 5.0 convolution_bitcast_fusion.3
  407.7 6.1 %fusion.64 = f32[768,64]{0,1:T(8,128)} fusion(f32[2,256,768]{2,1,0:T(8,128)} %fusion.163, f32[2,256,768]{2,1,0:T(8,128)} %copy-done.2, f32[2,256]{1,0:T(2,128)S(1)} %copy-done.64, bf16[1,1024,64]{1,2,0:T(8,128)(2,1)S(1)} %copy-done.16, bf16[1,1024,64]{1,2,0:T(8,128)(2,1)S(1)} %get-tuple-element.90), kind=kOutput, calls=%fused_computation.100 | convolution fusion | flops 53118208 | bytes 6754304 | tf_op jit(solution)/shard_map/jik,jid->kd/dot_general | solution.py:108
  417.5 7.0 %all-to-all-start.6 = ((bf16[16,64,1024]{2,1,0:T(8,128)(2,1)}), bf16[16,64,1024]{2,1,0:T(8,128)(2,1)S(1)}, u32[]{:S(2)}, u32[]{:S(2)}) async-start(bf16[16,64,1024]{2,1,0:T(8,128)(2,1)} %bitcast.197), calls=%async_computation.6 | async-start | bytes 4194304 | tf_op jit(solution)/shard_map/all_to_all | solution.py:154
  424.5 2.2 fusion.78
  426.7 1.7 maximum_convert_fusion
  428.4 1.6 convolution_bitcast_fusion.2
  430.0 2.0 convolution_bitcast_fusion.1
  432.0 2.0 convolution_bitcast_fusion
  434.1 5.7 convolution_convert_fusion.8
  439.7 6.0 %fusion.70 = bf16[2,256,64]{1,2,0:T(8,128)(2,1)} fusion(f32[2,256,768]{2,1,0:T(8,128)} %fusion.163, f32[2,256,768]{2,1,0:T(8,128)} %copy-done.2, f32[2,256]{1,0:T(2,128)} %log_add_fusion.1, bf16[1024,64]{0,1:T(8,128)(2,1)} %copy-done.36), kind=kOutput, calls=%fused_computation.104 | convolution fusion | flops 53118208 | bytes 6459392 | tf_op jit(solution)/shard_map/jik,kd->jid/dot_general | solution.py:106
  445.7 6.2 %fusion.67 = bf16[2,256,64]{1,2,0:T(8,128)(2,1)} fusion(f32[2,256,768]{2,1,0:T(8,128)} %fusion.164, f32[2,256,768]{2,1,0:T(8,128)} %copy-done.4, f32[2,256]{1,0:T(2,128)S(1)} %copy-done.67, bf16[1024,64]{0,1:T(8,128)(2,1)} %copy-done.36), kind=kOutput, calls=%fused_computation.103 | convolution fusion | flops 53118208 | bytes 6459392 | tf_op jit(solution)/shard_map/jik,kd->jid/dot_general | solution.py:106
  451.9 1.6 fusion.169
  453.5 1.7 fusion.223
  456.5 6.7 %all-to-all-start.7 = ((bf16[16,64,1024]{2,1,0:T(8,128)(2,1)}), bf16[16,64,1024]{2,1,0:T(8,128)(2,1)}, u32[]{:S(2)}, u32[]{:S(2)}) async-start(bf16[16,64,1024]{2,1,0:T(8,128)(2,1)} %bitcast.196), calls=%async_computation.7 | async-start | bytes 4194304 | tf_op jit(solution)/shard_map/all_to_all | solution.py:154
  463.3 1.6 convolution_convert_fusion.12
  470.3 18.0 %all-to-all-done.7 = bf16[16,64,1024]{2,1,0:T(8,128)(2,1)} async-done(((bf16[16,64,1024]{2,1,0:T(8,128)(2,1)}), bf16[16,64,1024]{2,1,0:T(8,128)(2,1)}, u32[]{:S(2)}, u32[]{:S(2)}) %all-to-all-start.7) | async-done | bytes 2097184 | tf_op jit(solution)/shard_map/all_to_all | solution.py:154
  488.3 7.9 %all-to-all-start.3 = ((bf16[16,64,384]{2,1,0:T(8,128)(2,1)}), bf16[16,64,384]{2,1,0:T(8,128)(2,1)S(1)}, u32[]{:S(2)}, u32[]{:S(2)}) async-start(bf16[16,64,384]{2,1,0:T(8,128)(2,1)} %pad_maximum_fusion.7), calls=%async_computation.3 | async-start | bytes 1572864 | tf_op jit(solution)/shard_map/all_to_all | solution.py:154
  496.2 3.2 fusion.60
  499.4 6.5 %all-to-all-done.3 = bf16[16,64,384]{2,1,0:T(8,128)(2,1)S(1)} async-done(((bf16[16,64,384]{2,1,0:T(8,128)(2,1)}), bf16[16,64,384]{2,1,0:T(8,128)(2,1)S(1)}, u32[]{:S(2)}, u32[]{:S(2)}) %all-to-all-start.3) | async-done | bytes 786464 | tf_op jit(solution)/shard_map/all_to_all | solution.py:154
  505.9 6.4 %all-to-all-start.5 = ((bf16[16,8,1024]{2,1,0:T(8,128)(2,1)}), bf16[16,8,1024]{2,1,0:T(8,128)(2,1)S(1)}, u32[]{:S(2)}, u32[]{:S(2)}) async-start(bf16[16,8,1024]{2,1,0:T(8,128)(2,1)} %fusion.60), calls=%async_computation.5 | async-start | bytes 524288 | tf_op jit(solution)/shard_map/all_to_all | solution.py:154
  514.4 2.2 all-to-all-done.5
  516.6 7.1 %all-to-all-start.4 = ((f32[8,8,384]{2,1,0:T(8,128)}), f32[8,8,384]{2,1,0:T(8,128)S(1)}, u32[]{:S(2)}, u32[]{:S(2)}) async-start(f32[8,8,384]{2,1,0:T(8,128)} %bitcast.59), calls=%async_computation.4 | async-start | bytes 196608 | tf_op jit(solution)/shard_map/all_to_all | solution.py:317
  523.7 2.2 convolution_convert_fusion.4
  525.9 2.8 all-to-all-done.4
  528.7 4.3 all-to-all-start.2
  535.1 2.0 convert_reduce_fusion.2
  537.2 2.0 convert_reduce_fusion.1
  539.8 4.8 collective-permute-start
  546.6 14.4 %collective-permute-done = f32[8,1024]{1,0:T(8,128)S(1)} collective-permute-done((f32[8,1024]{1,0:T(8,128)}, f32[8,1024]{1,0:T(8,128)S(1)}, u32[]{:S(2)}, u32[]{:S(2)}) %collective-permute-start) | collective-permute-done | bytes 32800 | tf_op jit(solution)/shard_map/ppermute | solution.py:289
  (327 shorter events, 77.1 us)
Async XLA Ops:
  7.2 37.1 %all-gather.9.cloned.1.call-start = ((), (), s32[]{:S(2)}) async-start(), calls=%async_computation.11 | async-start | bytes 2359296 | tf_op jit(solution)/shard_map/all_gather | solution.py:172
  13.6 10.8 %all-to-all-start = ((bf16[8,8,384]{2,1,0:T(8,128)(2,1)}), bf16[8,8,384]{2,1,0:T(8,128)(2,1)S(1)}, u32[]{:S(2)}, u32[]{:S(2)}) async-start(bf16[8,8,384]{2,1,0:T(8,128)(2,1)} %maximum_bitcast_fusion), calls=%async_computation | async-start | bytes 98304 | tf_op jit(solution)/shard_map/all_to_all | solution.py:168
  19.6 63.7 %all-gather.21.cloned.1.call-start = ((), (), s32[]{:S(2)}) async-start(), calls=%async_computation.17 | async-start | bytes 2359296 | tf_op jit(solution)/shard_map/all_gather | solution.py:204
  47.5 5.5 copy-start.37
  47.8 4.2 copy-start.36
  48.6 5.3 copy-start.28
  53.9 33.5 %copy-start.34 = (bf16[256,128]{1,0:T(8,128)(2,1)}, bf16[256,128]{1,0:T(8,128)(2,1)S(1)}, u32[]{:S(2)}) copy-start(bf16[256,128]{1,0:T(8,128)(2,1)S(1)} %copy.139) | copy-start | bytes 196612
  54.7 95.4 %all-gather.11.cloned.1.call-start = ((), (), s32[]{:S(2)}) async-start(), calls=%async_computation.12 | async-start | bytes 2113536 | tf_op jit(solution)/shard_map/all_gather | solution.py:177
  55.4 124.9 %all-gather.13.cloned.1.call-start = ((), (), s32[]{:S(2)}) async-start(), calls=%async_computation.13 | async-start | bytes 2654208 | tf_op jit(solution)/shard_map/all_gather | solution.py:176
  56.9 176.1 %all-gather.15.cloned.1.call-start = ((), (), s32[]{:S(2)}) async-start(), calls=%async_computation.14 | async-start | bytes 4456448 | tf_op jit(solution)/shard_map/all_gather | solution.py:178
  57.5 220.6 %all-gather.17.cloned.1.call-start = ((), (), s32[]{:S(2)}) async-start(), calls=%async_computation.15 | async-start | bytes 2228224 | tf_op jit(solution)/shard_map/all_gather | solution.py:179
  83.3 66.7 %copy-start.13 = (bf16[1024,1024]{0,1:T(8,128)(2,1)S(1)}, bf16[1024,1024]{0,1:T(8,128)(2,1)}, u32[]{:S(2)}) copy-start(bf16[1024,1024]{0,1:T(8,128)(2,1)} %all-gather.9.cloned.1.call-done) | copy-start | bytes 6291460
  182.5 102.3 %copy-start.76 = (f32[1024]{0:T(1024)}, f32[1024]{0:T(1024)S(1)}, u32[]{:S(2)}) copy-start(f32[1024]{0:T(1024)S(1)} %broadcast_multiply_fusion.1) | copy-start | bytes 12292
  182.5 95.6 %copy-start.75 = (f32[1024]{0:T(1024)}, f32[1024]{0:T(1024)S(1)}, u32[]{:S(2)}) copy-start(f32[1024]{0:T(1024)S(1)} %broadcast_multiply_fusion) | copy-start | bytes 12292
  233.0 6.1 %copy-start.81 = (bf16[2,1024,1024]{2,1,0:T(8,128)(2,1)S(1)}, bf16[2,1024,1024]{2,1,0:T(8,128)(2,1)}, u32[]{:S(2)}) copy-start(bf16[2,1024,1024]{2,1,0:T(8,128)(2,1)} %all-gather.15.cloned.1.call-done) | copy-start | bytes 12582916
  278.1 5.4 copy-start.83
  283.5 13.0 %copy-start.89 = (bf16[1024,512]{0,1:T(8,128)(2,1)}, bf16[1024,512]{0,1:T(8,128)(2,1)S(1)}, u32[]{:S(2)}) copy-start(bf16[1024,512]{0,1:T(8,128)(2,1)S(1)} %get-tuple-element.80) | copy-start | bytes 3145732
  283.5 13.0 %copy-start.91 = (bf16[1024,512]{0,1:T(8,128)(2,1)}, bf16[1024,512]{0,1:T(8,128)(2,1)S(1)}, u32[]{:S(2)}) copy-start(bf16[1024,512]{0,1:T(8,128)(2,1)S(1)} %get-tuple-element.81) | copy-start | bytes 3145732
  300.7 35.2 %all-to-all-start.1 = ((bf16[8,128,1152]{2,1,0:T(8,128)(2,1)}), bf16[8,128,1152]{2,1,0:T(8,128)(2,1)}, u32[]{:S(2)}, u32[]{:S(2)}) async-start(bf16[8,128,1152]{2,1,0:T(8,128)(2,1)} %pad_maximum_fusion), calls=%async_computation.1 | async-start | bytes 4718592 | tf_op jit(solution)/shard_map/all_to_all | solution.py:154
  306.6 74.9 %all-gather.19.cloned.1.call-start = ((), (), s32[]{:S(2)}) async-start(), calls=%async_computation.16 | async-start | bytes 2359296 | tf_op jit(solution)/shard_map/all_gather | solution.py:271
  355.0 31.5 %all-to-all-start.8 = ((bf16[16,64,512]{2,1,0:T(8,128)(2,1)}), bf16[16,64,512]{2,1,0:T(8,128)(2,1)}, u32[]{:S(2)}, u32[]{:S(2)}) async-start(bf16[16,64,512]{2,1,0:T(8,128)(2,1)} %bitcast.202), calls=%async_computation.8 | async-start | bytes 2097152 | tf_op jit(solution)/shard_map/all_to_all | solution.py:154
  361.7 183.8 %reduce-scatter.4.cloned.1.call-start = ((), (), s32[]{:S(2)}) async-start(), calls=%async_computation.18 | async-start | bytes 2359296
  365.9 5.5 copy-start.90
  365.9 5.5 copy-start.92
  375.3 5.2 copy-start.68
  383.6 31.8 %copy-start.11 = (bf16[1024,128]{0,1:T(8,128)(2,1)}, bf16[1024,128]{0,1:T(8,128)(2,1)S(1)}, u32[]{:S(2)}) copy-start(bf16[1024,128]{0,1:T(8,128)(2,1)S(1)} %convolution_convert_fusion.6) | copy-start | bytes 786436
  384.9 8.4 %copy-start.42 = (bf16[2,256,64]{1,2,0:T(8,128)(2,1)S(1)}, bf16[2,256,64]{1,2,0:T(8,128)(2,1)}, u32[]{:S(2)}) copy-start(bf16[2,256,64]{1,2,0:T(8,128)(2,1)} %copy-done.41) | copy-start | bytes 196612
  384.9 8.4 %copy-start.65 = (f32[2,256]{1,0:T(2,128)S(1)}, f32[2,256]{1,0:T(2,128)}, u32[]{:S(2)}) copy-start(f32[2,256]{1,0:T(2,128)} %log_add_fusion) | copy-start | bytes 6148
  386.5 14.6 %copy-start.16 = (bf16[1,1024,64]{1,2,0:T(8,128)(2,1)S(1)}, bf16[1,1024,64]{1,2,0:T(8,128)(2,1)}, u32[]{:S(2)}) copy-start(bf16[1,1024,64]{1,2,0:T(8,128)(2,1)} %copy-done.15) | copy-start | bytes 393220
  386.5 14.6 %copy-start.63 = (f32[2,256]{1,0:T(2,128)S(1)}, f32[2,256]{1,0:T(2,128)}, u32[]{:S(2)}) copy-start(f32[2,256]{1,0:T(2,128)} %log_add_fusion.2) | copy-start | bytes 6148
  386.5 29.9 %all-to-all-start.9 = ((bf16[16,64,512]{2,1,0:T(8,128)(2,1)}), bf16[16,64,512]{2,1,0:T(8,128)(2,1)S(1)}, u32[]{:S(2)}, u32[]{:S(2)}) async-start(bf16[16,64,512]{2,1,0:T(8,128)(2,1)} %bitcast.203), calls=%async_computation.9 | async-start | bytes 2097152 | tf_op jit(solution)/shard_map/all_to_all | solution.py:154
  399.6 8.1 %copy-start.64 = (f32[2,256]{1,0:T(2,128)S(1)}, f32[2,256]{1,0:T(2,128)}, u32[]{:S(2)}) copy-start(f32[2,256]{1,0:T(2,128)} %log_add_fusion.1) | copy-start | bytes 6148
  406.1 7.7 %copy-start.53 = (f32[512,64]{0,1:T(8,128)}, f32[512,64]{0,1:T(8,128)S(1)}, u32[]{:S(2)}) copy-start(f32[512,64]{0,1:T(8,128)S(1)} %convolution_bitcast_fusion.3) | copy-start | bytes 393220
  416.5 8.0 %copy-start.62 = (f32[2,256]{1,0:T(2,128)S(1)}, f32[2,256]{1,0:T(2,128)}, u32[]{:S(2)}) copy-start(f32[2,256]{1,0:T(2,128)} %log_add_fusion.3) | copy-start | bytes 6148
  417.5 37.7 %all-to-all-start.6 = ((bf16[16,64,1024]{2,1,0:T(8,128)(2,1)}), bf16[16,64,1024]{2,1,0:T(8,128)(2,1)S(1)}, u32[]{:S(2)}, u32[]{:S(2)}) async-start(bf16[16,64,1024]{2,1,0:T(8,128)(2,1)} %bitcast.197), calls=%async_computation.6 | async-start | bytes 4194304 | tf_op jit(solution)/shard_map/all_to_all | solution.py:154
  426.7 5.3 copy-start.5
  426.7 5.3 copy-start.66
  439.7 6.0 %copy-start.67 = (f32[2,256]{1,0:T(2,128)S(1)}, f32[2,256]{1,0:T(2,128)}, u32[]{:S(2)}) copy-start(f32[2,256]{1,0:T(2,128)} %log_add_fusion) | copy-start | bytes 6148
  456.5 31.7 %all-to-all-start.7 = ((bf16[16,64,1024]{2,1,0:T(8,128)(2,1)}), bf16[16,64,1024]{2,1,0:T(8,128)(2,1)}, u32[]{:S(2)}, u32[]{:S(2)}) async-start(bf16[16,64,1024]{2,1,0:T(8,128)(2,1)} %bitcast.196), calls=%async_computation.7 | async-start | bytes 4194304 | tf_op jit(solution)/shard_map/all_to_all | solution.py:154
  463.2 4.9 copy-start.19
  463.2 4.9 copy-start.21
  463.2 4.9 copy-start.22
  463.2 4.9 copy-start.23
  463.2 4.9 copy-start.24
  463.2 4.9 copy-start.25
  463.2 4.9 copy-start.26
  463.3 4.9 copy-start.39
  469.2 27.0 %copy-start.29 = (bf16[256,128]{1,0:T(8,128)(2,1)S(1)}, bf16[256,128]{1,0:T(8,128)(2,1)}, u32[]{:S(2)}) copy-start(bf16[256,128]{1,0:T(8,128)(2,1)} %copy-done.28) | copy-start | bytes 196612
  469.2 27.0 %copy-start.31 = (bf16[256,128]{1,0:T(8,128)(2,1)S(1)}, bf16[256,128]{1,0:T(8,128)(2,1)}, u32[]{:S(2)}) copy-start(bf16[256,128]{1,0:T(8,128)(2,1)} %copy-done.30) | copy-start | bytes 196612
  469.2 27.0 %copy-start.33 = (bf16[256,128]{1,0:T(8,128)(2,1)S(1)}, bf16[256,128]{1,0:T(8,128)(2,1)}, u32[]{:S(2)}) copy-start(bf16[256,128]{1,0:T(8,128)(2,1)} %copy-done.32) | copy-start | bytes 196612
  469.2 27.0 %copy-start.35 = (bf16[256,128]{1,0:T(8,128)(2,1)S(1)}, bf16[256,128]{1,0:T(8,128)(2,1)}, u32[]{:S(2)}) copy-start(bf16[256,128]{1,0:T(8,128)(2,1)} %copy-done.34) | copy-start | bytes 196612
  488.3 17.6 %all-to-all-start.3 = ((bf16[16,64,384]{2,1,0:T(8,128)(2,1)}), bf16[16,64,384]{2,1,0:T(8,128)(2,1)S(1)}, u32[]{:S(2)}, u32[]{:S(2)}) async-start(bf16[16,64,384]{2,1,0:T(8,128)(2,1)} %pad_maximum_fusion.7), calls=%async_computation.3 | async-start | bytes 1572864 | tf_op jit(solution)/shard_map/all_to_all | solution.py:154
  496.2 27.5 %copy-start.10 = (bf16[1024,384]{1,0:T(8,128)(2,1)S(1)}, bf16[1024,384]{1,0:T(8,128)(2,1)}, u32[]{:S(2)}) copy-start(bf16[1024,384]{1,0:T(8,128)(2,1)} %copy-done.9) | copy-start | bytes 2359300
  496.2 27.5 %copy-start.44 = (bf16[256,64]{0,1:T(8,128)(2,1)S(1)}, bf16[256,64]{0,1:T(8,128)(2,1)}, u32[]{:S(2)}) copy-start(bf16[256,64]{0,1:T(8,128)(2,1)} %get-tuple-element.105) | copy-start | bytes 98308
  499.4 24.3 %copy-start.46 = (bf16[256,64]{0,1:T(8,128)(2,1)S(1)}, bf16[256,64]{0,1:T(8,128)(2,1)}, u32[]{:S(2)}) copy-start(bf16[256,64]{0,1:T(8,128)(2,1)} %get-tuple-element.106) | copy-start | bytes 98308
  499.4 24.3 %copy-start.48 = (bf16[256,64]{0,1:T(8,128)(2,1)S(1)}, bf16[256,64]{0,1:T(8,128)(2,1)}, u32[]{:S(2)}) copy-start(bf16[256,64]{0,1:T(8,128)(2,1)} %copy-done.47) | copy-start | bytes 98308
  499.4 24.3 %copy-start.50 = (bf16[256,64]{0,1:T(8,128)(2,1)S(1)}, bf16[256,64]{0,1:T(8,128)(2,1)}, u32[]{:S(2)}) copy-start(bf16[256,64]{0,1:T(8,128)(2,1)} %copy-done.49) | copy-start | bytes 98308
  505.9 10.7 %all-to-all-start.5 = ((bf16[16,8,1024]{2,1,0:T(8,128)(2,1)}), bf16[16,8,1024]{2,1,0:T(8,128)(2,1)S(1)}, u32[]{:S(2)}, u32[]{:S(2)}) async-start(bf16[16,8,1024]{2,1,0:T(8,128)(2,1)} %fusion.60), calls=%async_computation.5 | async-start | bytes 524288 | tf_op jit(solution)/shard_map/all_to_all | solution.py:154
  516.6 12.1 %all-to-all-start.4 = ((f32[8,8,384]{2,1,0:T(8,128)}), f32[8,8,384]{2,1,0:T(8,128)S(1)}, u32[]{:S(2)}, u32[]{:S(2)}) async-start(f32[8,8,384]{2,1,0:T(8,128)} %bitcast.59), calls=%async_computation.4 | async-start | bytes 196608 | tf_op jit(solution)/shard_map/all_to_all | solution.py:317
  528.7 41.8 %all-to-all-start.2 = ((bf16[8,128,1024]{2,1,0:T(8,128)(2,1)}), bf16[8,128,1024]{2,1,0:T(8,128)(2,1)S(1)}, u32[]{:S(2)}, u32[]{:S(2)}) async-start(bf16[8,128,1024]{2,1,0:T(8,128)(2,1)} %bitcast.198), calls=%async_computation.2 | async-start | bytes 4194304 | tf_op jit(solution)/shard_map/all_to_all | solution.py:154
  537.1 31.3 %copy-start.40 = (bf16[8,2048]{1,0:T(8,128)(2,1)S(1)}, bf16[8,2048]{1,0:T(8,128)(2,1)}, u32[]{:S(2)}) copy-start(bf16[8,2048]{1,0:T(8,128)(2,1)} %param.18) | copy-start | bytes 98308
  537.2 32.8 %copy-start.79 = (bf16[8]{0:T(256)(128)(2,1)S(1)}, bf16[8]{0:T(256)(128)(2,1)}, u32[]{:S(2)}) copy-start(bf16[8]{0:T(256)(128)(2,1)} %param.17) | copy-start | bytes 52
  539.8 21.1 %collective-permute-start = (f32[8,1024]{1,0:T(8,128)}, f32[8,1024]{1,0:T(8,128)S(1)}, u32[]{:S(2)}, u32[]{:S(2)}) collective-permute-start(f32[8,1024]{1,0:T(8,128)} %convert_reduce_fusion.7), channel_id=1, source_target_pairs={{0,0},{1,16},{2,32},{3,48},{4,64},{5,80},{6,96},{7,112},{8,1},{9,1... | collective-permute-start | bytes 98312 | tf_op jit(solution)/shard_map/ppermute | solution.py:289
  562.3 10.6 %copy-start.6 = (bf16[128,1024]{0,1:T(8,128)(2,1)S(1)}, bf16[128,1024]{0,1:T(8,128)(2,1)}, u32[]{:S(2)}) copy-start(bf16[128,1024]{0,1:T(8,128)(2,1)} %copy.130) | copy-start | bytes 786436
  (48 other events, 98.1 us)
Sparse Core Ops, SparseCore 0:
  10.3 30.0 all-gather.8
  54.8 28.5 all-gather.20
  86.5 63.5 all-gather.10
  152.1 28.1 all-gather.12
  182.3 50.5 all-gather.14
  235.0 43.0 all-gather.16
  346.0 27.3 all-gather.18
  375.8 31.4 reduce-scatter.3
